TPU v7x, 512 devices: a whole 4x8x8 slice. The times are simulated.
512 devices in a mesh: row: 16 (over x, z_hi), col: 32 (over z_lo, y, core).
Axes of the slice: x: 4, y: 8, z: 8 (z_hi: 4, z_lo: 2; z = z_hi * 2 + z_lo), core: 2. Of those that a mesh axis runs over, the one named last changes fastest.
Arguments:
- bin_features: bfloat16 [4096, 512], P('row'), may hold values from -6 to 6
- w_left: bfloat16 [512, 32], replicated, may hold values from -0.25 to 0.25
- w_right: bfloat16 [512, 32], replicated, may hold values from -0.25 to 0.25
- depth_kernel: float32 [9, 32], replicated, may hold values from -2 to 2
- w_point: bfloat16 [32, 32], replicated, may hold values from -1 to 1
- w_head: bfloat16 [32, 24], replicated, may hold values from -1 to 1
- cotangent: bfloat16 [24, 4096, 4096], P(None, 'row', 'col'), may hold values from -6 to 6
Outputs:
- grad_features: bfloat16 [4096, 512], P('row')
- grad_w_left: float32 [512, 32], replicated
- grad_w_right: float32 [512, 32], replicated
- grad_kernel: float32 [9, 32], replicated
- grad_point: float32 [32, 32], replicated
- grad_head: float32 [32, 24], replicated
All inputs are finite; a program needn't handle non-finite values.
Results may differ from a plain program's by a relative error of at most 0.019.
Values may be sent and summed in bfloat16 or wider, within the bound.
No kernel may reach another device: no remote copies, remote signals or barrier semaphores. Data moves between devices by JAX's collectives and lax.ppermute only.
A program may use at most 64 MiB of HBM per device.

v0:
```python
import math
import jax
import jax.numpy as jnp
from jax import lax
from jax.sharding import PartitionSpec as P

DILATION_STEP = 4


def from_root(block, axis, source):
    block = jnp.where(lax.axis_index(axis) == source, block, jnp.zeros_like(block))
    return lax.psum(block, axis)


def extended(x, sides, width):
    for axis, dim in sides:
        count, length = (lax.axis_size(axis), x.shape[dim])
        up = [(i, (i + 1) % count) for i in range(count - 1)]
        down = [(j, i) for i, j in up]
        last = lax.slice_in_dim(x, length - width, length, axis=dim)
        first = lax.slice_in_dim(x, 0, width, axis=dim)
        before = lax.ppermute(last, axis, up)
        after = lax.ppermute(first, axis, down)
        x = jnp.concatenate([before, x, after], axis=dim)
    return x


def silu_slope(values):
    logistic = jax.nn.sigmoid(values)
    return logistic * (1.0 + values * (1.0 - logistic))


def depthwise(kernel_taps, padded, output_rows, output_columns):
    result = jnp.zeros((padded.shape[0], output_rows, output_columns), jnp.float32)
    for kernel_tap_row in range(3):
        for kernel_tap_column in range(3):
            result = result + kernel_taps[3 * kernel_tap_row + kernel_tap_column][
                :, None, None
            ] * padded[
                :,
                DILATION_STEP * kernel_tap_row : DILATION_STEP * kernel_tap_row + output_rows,
                DILATION_STEP * kernel_tap_column : DILATION_STEP * kernel_tap_column
                + output_columns,
            ].astype(
                jnp.float32
            )
    return result


def body(bin_features, w_left, w_right, depth_kernel, w_point, w_head, cotangent):
    rows_per_tile = bin_features.shape[0]
    columns_per_tile = cotangent.shape[2]
    chans = w_left.shape[1]
    row_count = lax.axis_size("row")
    col_count = lax.axis_size("col")
    panel_ratio = col_count // row_count
    contact_map_bins = rows_per_tile * row_count
    grad_scale = 1.0 / math.sqrt(contact_map_bins)
    row_index = lax.axis_index("row")
    col_index = lax.axis_index("col")
    left_panel = jnp.dot(bin_features, w_left, preferred_element_type=jnp.float32).astype(
        jnp.bfloat16
    )
    offset = col_index % panel_ratio * columns_per_tile
    own_rows = lax.dynamic_slice_in_dim(bin_features, offset, columns_per_tile, 0)
    right_own = jnp.dot(own_rows, w_right, preferred_element_type=jnp.float32).astype(jnp.bfloat16)
    right_panel = from_root(right_own, "row", col_index // panel_ratio)
    pair_matrix = (
        left_panel.astype(jnp.float32).T[:, :, None] + right_panel.astype(jnp.float32).T[:, None, :]
    ).astype(jnp.bfloat16)
    extended_pair = extended(pair_matrix, (("row", 1), ("col", 2)), DILATION_STEP)
    convolved_map = depthwise(depth_kernel, extended_pair, rows_per_tile, columns_per_tile)
    trunk_gradient = (
        grad_scale
        * jnp.einsum("ch,hij->cij", w_head, cotangent, preferred_element_type=jnp.float32)
    ).astype(jnp.bfloat16)
    grad_hidden = jnp.einsum(
        "co,oij->cij", w_point, trunk_gradient, preferred_element_type=jnp.float32
    )
    convolved_gradient = (grad_hidden * silu_slope(convolved_map)).astype(jnp.bfloat16)
    extended_gradient = extended(convolved_gradient, (("row", 1), ("col", 2)), DILATION_STEP)
    hidden_state = jax.nn.silu(convolved_map).astype(jnp.bfloat16)
    mixed_out = jnp.einsum("co,cij->oij", w_point, hidden_state, preferred_element_type=jnp.float32)
    centre_offset = extended_pair[
        :,
        DILATION_STEP : DILATION_STEP + rows_per_tile,
        DILATION_STEP : DILATION_STEP + columns_per_tile,
    ]
    trunk_matrix = (centre_offset.astype(jnp.float32) + mixed_out).astype(jnp.bfloat16)
    conv_f32 = convolved_gradient.astype(jnp.float32)
    backward_pass = jnp.zeros((chans, rows_per_tile, columns_per_tile), jnp.float32)
    kern_terms = []
    for kernel_tap_row in range(3):
        for kernel_tap_column in range(3):
            backward_pass = backward_pass + depth_kernel[3 * kernel_tap_row + kernel_tap_column][
                :, None, None
            ] * extended_gradient[
                :,
                DILATION_STEP * (2 - kernel_tap_row) : DILATION_STEP * (2 - kernel_tap_row)
                + rows_per_tile,
                DILATION_STEP * (2 - kernel_tap_column) : DILATION_STEP * (2 - kernel_tap_column)
                + columns_per_tile,
            ].astype(
                jnp.float32
            )
            shifted_window = extended_pair[
                :,
                DILATION_STEP * kernel_tap_row : DILATION_STEP * kernel_tap_row + rows_per_tile,
                DILATION_STEP * kernel_tap_column : DILATION_STEP * kernel_tap_column
                + columns_per_tile,
            ].astype(jnp.float32)
            kern_terms.append(jnp.sum(conv_f32 * shifted_window, axis=(1, 2)))
    kernel_part = jnp.stack(kern_terms)
    pair_gradient = trunk_gradient.astype(jnp.float32) + backward_pass
    left_part = jnp.sum(pair_gradient, axis=2).T
    right_part = jnp.sum(pair_gradient, axis=1).T
    point_part = jnp.einsum(
        "fsk,gsk->fg", hidden_state, trunk_gradient, preferred_element_type=jnp.float32
    )
    head_part = jnp.einsum(
        "ydq,gdq->yg", trunk_matrix, cotangent, preferred_element_type=jnp.float32
    )
    grad_left = lax.psum(left_part, "col").astype(jnp.bfloat16)
    column_total = lax.psum(right_part, "row").astype(jnp.bfloat16)
    all_panels = lax.all_gather(column_total, "col", axis=0, tiled=True)
    grad_right = lax.dynamic_slice_in_dim(all_panels, row_index * rows_per_tile, rows_per_tile, 0)
    grad_features = (
        jnp.dot(grad_left, w_left.T, preferred_element_type=jnp.float32)
        + jnp.dot(grad_right, w_right.T, preferred_element_type=jnp.float32)
    ).astype(jnp.bfloat16)
    contract = (((0,), (0,)), ((), ()))
    wleft_part = lax.dot_general(
        bin_features, grad_left, contract, preferred_element_type=jnp.float32
    )
    wright_part = lax.dot_general(
        bin_features, grad_right, contract, preferred_element_type=jnp.float32
    )
    kernel_sum, point_sum, head_sum = lax.psum((kernel_part, point_part, head_part), ("row", "col"))
    wleft_sum, wright_sum = lax.psum((wleft_part, wright_part), "row")
    return (
        grad_features,
        grad_scale * wleft_sum,
        grad_scale * wright_sum,
        grad_scale * kernel_sum,
        grad_scale * point_sum,
        grad_scale * head_sum,
    )


def solution(mesh):
    placed = (P("row", None), P(), P(), P(), P(), P(), P(None, "row", "col"))
    return jax.shard_map(
        body,
        mesh=mesh,
        in_specs=placed,
        out_specs=(P("row", None), P(), P(), P(), P(), P()),
        check_vma=False,
    )
```

profile of v0, /device:TPU:8, one launch (start us, length us, event | category | flops | bytes accessed | tf_op | source)
XLA Modules:
  0.0 674.3 jit_solution(18254187634809960480)
XLA Ops:
  8.4 50.8 %psum.56 = bf16[32,128]{1,0:T(8,128)(2,1)S(1)} all-reduce(bf16[32,128]{1,0:T(8,128)(2,1)S(1)} %fusion.34), channel_id=1, replica_groups=mesh['row'=16,'col'=32] {'row'}, use_global_device_ids=true, to_apply=%region_0.1 | all-reduce | flops 4096 | bytes 16384 | tf_op jit(solution)/shard_map/psum | solution.py:12
  64.8 3.5 multiply_convert_fusion.1
  68.3 1.9 collective-permute-done.1
  70.5 2.9 fusion.51
  73.5 3.6 copy.20
  77.1 3.6 copy.22
  80.8 1.9 collective-permute-start.3
  82.7 2.6 collective-permute-start.2
  85.3 3.3 collective-permute-done.2
  88.6 3.0 copy.21
  91.6 3.0 copy.23
  94.7 7.2 %maximum_maximum_fusion = (bf16[32,264,132]{2,0,1:T(8,128)(2,1)S(1)}, bf16[32,264,132]{2,0,1:T(8,128)(2,1)S(1)}) fusion(bf16[32,4,128]{2,0,1:T(8,128)(2,1)S(1)} %collective-permute-done.1, bf16[32,256,128]{2,0,1:T(8,128)(2,1)} %copy-done.1, bf16[32,4,128]{2,0,1:T(8,128)(2,1)S(1)} %collective-permute-done, bf16[32,264,4]{2,0,1:T(8,128)(2,1)} %copy.21, ...), kind=kLoop, calls=%fused_computation.20 | loop fusion | flops 17842176 | bytes 6758400 | tf_op jit(solution)/shard_map/concatenate | solution.py:24
  101.9 10.2 %multiply_convert_fusion = (bf16[32,256,128]{2,0,1:T(8,128)(2,1)}, f32[32,256,128]{2,0,1:T(8,128)}) fusion(bf16[32,264,132]{2,0,1:T(8,128)(2,1)S(1)} %get-tuple-element.34, f32[32]{0:T(128)S(1)} %get-tuple-element.48, bf16[32,4,128]{2,0,1:T(8,128)(2,1)S(1)} %collective-permute-done.1, bf16[32,256,128]{2,0,1:T(8,128)(2,1)S(1)} %copy-done.2, ...), kind=kLoop, calls=%fused_computation.50 | loop fusion | flops 36700160 | bytes 21087360 | tf_op jit(solution)/shard_map/convert_element_type | solution.py:82
  112.1 3.4 fusion.30
  115.6 3.0 convolution_bitcast_fusion.2
  119.0 13.2 %fusion.23 = (f32[32]{0:T(128)S(1)}, f32[32]{0:T(128)S(1)}, f32[32]{0:T(128)S(1)}, f32[32]{0:T(128)S(1)}, f32[32]{0:T(128)S(1)}, /*index=5*/f32[32]{0:T(128)S(1)...) fusion(bf16[32,264,132]{2,0,1:T(8,128)(2,1)} %copy-done.5, ...), kind=kOutput, calls=%fused_computation.47 | convolution fusion | flops 110100192 | bytes 23186560 | tf_op jit(solution)/shard_map/co,oij->cij/dot_general | solution.py:77
  132.3 96.0 %all-reduce = (f32[9,32]{1,0:T(8,128)S(1)}, f32[32,32]{1,0:T(8,128)S(1)}, f32[32,24]{0,1:T(8,128)S(1)}) all-reduce(f32[9,32]{1,0:T(8,128)S(1)} %stack.39, f32[32,32]{1,0:T(8,128)S(1)} %convolution_bitcast_fusion.2, f32[32,24]{0,1:T(8,128)S(1)} %fusion.30), channel_id=1, replica_groups=mesh['row'=16,'col'=32] {'row','col'}, use_global_device_ids=true, to_apply=%region_16.17 | all-reduce | flops 2080 | bytes 16640 | tf_op jit(solution)/shard_map/psum | solution.py:138
  229.7 2.8 collective-permute-start.4
  234.6 5.1 collective-permute-done.5
  241.5 2.9 fusion.50
  244.5 3.6 copy.24
  248.1 3.6 copy.26
  251.8 1.9 collective-permute-start.7
  253.7 3.6 collective-permute-start.6
  259.5 3.0 copy.25
  262.6 3.0 copy.27
  265.6 7.2 %pad_maximum_fusion.1 = (bf16[32,264,132]{2,0,1:T(8,128)(2,1)S(1)}, bf16[32,264,132]{2,0,1:T(8,128)(2,1)S(1)}) fusion(bf16[32,264,4]{2,0,1:T(8,128)(2,1)} %copy.25, bf16[32,4,128]{2,0,1:T(8,128)(2,1)S(1)} %collective-permute-done.5, bf16[32,256,128]{2,0,1:T(8,128)(2,1)} %get-tuple-element.50, bf16[32,4,128]{2,0,1:T(8,128)(2,1)S(1)} %collective-permute-done.4, ...), kind=kLoop, calls=%fused_computation.22 | loop fusion | flops 17842176 | bytes 6758400 | tf_op jit(solution)/shard_map/concatenate | solution.py:24
  272.9 7.2 %fusion.48 = (f32[32,128]{1,0:T(8,128)S(1)}, f32[32,256]{0,1:T(8,128)S(1)}) fusion(bf16[32,264,132]{2,0,1:T(8,128)(2,1)S(1)} %get-tuple-element.30, f32[32]{0:T(128)S(1)} %get-tuple-element.48, bf16[32,256,128]{2,0,1:T(8,128)(2,1)S(1)} %copy-done.6, bf16[32,4,128]{2,0,1:T(8,128)(2,1)S(1)} %collective-permute-done.4, f32[32]{0:T(128)S(1)} %get-tuple-element.49, ...), kind=kLoop, calls=%fused_computation.100 | loop fusion | flops 33542144 | bytes 16893056 | tf_op jit(solution)/shard_map/reduce_sum | solution.py:116
  280.2 102.3 %psum.57 = bf16[256,32]{1,0:T(8,128)(2,1)S(1)} all-reduce(f32[256,32]{1,0:T(8,128)S(1)} %bitcast.73), channel_id=1, replica_groups=mesh['row'=16,'col'=32] {'col'}, use_global_device_ids=true, to_apply=%region_2.3 | all-reduce | flops 8192 | bytes 49152 | tf_op jit(solution)/shard_map/psum | solution.py:123
  383.5 80.7 %psum.58 = bf16[128,32]{0,1:T(8,128)(2,1)S(1)} all-reduce(f32[128,32]{0,1:T(8,128)S(1)} %bitcast.74), channel_id=1, replica_groups=mesh['row'=16,'col'=32] {'row'}, use_global_device_ids=true, to_apply=%region_4.5 | all-reduce | flops 4096 | bytes 24576 | tf_op jit(solution)/shard_map/psum | solution.py:124
  464.2 35.4 %all_gather.3 = bf16[4096,32]{0,1:T(8,128)(2,1)S(1)} all-gather(bf16[128,32]{0,1:T(8,128)(2,1)S(1)} %psum.58), channel_id=1, replica_groups=mesh['row'=16,'col'=32] {'col'}, dimensions={0}, use_global_device_ids=true | all-gather | bytes 270336 | tf_op jit(solution)/shard_map/all_gather | solution.py:125
  501.3 164.6 %all-reduce.4.cloned.1.call-done = (f32[512,32]{0,1:T(8,128)}, f32[512,32]{0,1:T(8,128)}) async-done(((f32[512,32]{0,1:T(8,128)}, f32[512,32]{0,1:T(8,128)}), (f32[512,32]{0,1:T(8,128)}, f32[512,32]{0,1:T(8,128)})) %all-reduce.4.cloned.1.call-update) | async-done | bytes 131088 | tf_op jit(solution)/shard_map/psum | solution.py:139
  (57 shorter events, 19.4 us)
Async XLA Ops:
  7.2 57.7 %copy-start = (bf16[24,256,128]{2,1,0:T(8,128)(2,1)S(1)}, bf16[24,256,128]{2,1,0:T(8,128)(2,1)}, u32[]{:S(2)}) copy-start(bf16[24,256,128]{2,1,0:T(8,128)(2,1)} %param.13) | copy-start | bytes 4718596
  7.2 658.8 %all-reduce.4.cloned.1.call-start = ((), (), s32[]{:S(2)}) async-start(), calls=%async_computation | async-start | bytes 262144 | tf_op jit(solution)/shard_map/psum | solution.py:139
  62.2 8.0 %copy-start.1 = (bf16[32,256,128]{2,0,1:T(8,128)(2,1)}, bf16[32,256,128]{2,0,1:T(8,128)(2,1)S(1)}, u32[]{:S(2)}) copy-start(bf16[32,256,128]{2,0,1:T(8,128)(2,1)S(1)} %add_convert_fusion) | copy-start | bytes 6291460
  62.2 6.1 collective-permute-start
  63.5 6.7 collective-permute-start.1
  73.5 11.8 %copy-start.12 = (f32[9,32]{1,0:T(8,128)S(1)}, f32[9,32]{1,0:T(8,128)}, u32[]{:S(2)}) copy-start(f32[9,32]{1,0:T(8,128)} %param.10) | copy-start | bytes 3460
  80.8 10.9 %collective-permute-start.3 = (bf16[32,264,4]{1,0,2:T(8,128)(2,1)S(1)}, bf16[32,264,4]{1,0,2:T(8,128)(2,1)S(1)}, u32[]{:S(2)}, u32[]{:S(2)}) collective-permute-start(bf16[32,264,4]{1,0,2:T(8,128)(2,1)S(1)} %copy.22), channel_id=1, source_target_pairs={{1,0},{2,1},{3,2},{4,3},{5,4},{6,5},{7,6},{8,7},{9,8},{10,9},{11,1... | collective-permute-start | bytes 202760 | tf_op jit(solution)/shard_map/ppermute | solution.py:23
  82.7 5.9 collective-permute-start.2
  94.7 7.2 %copy-start.2 = (bf16[32,256,128]{2,0,1:T(8,128)(2,1)S(1)}, bf16[32,256,128]{2,0,1:T(8,128)(2,1)}, u32[]{:S(2)}) copy-start(bf16[32,256,128]{2,0,1:T(8,128)(2,1)} %copy-done.1) | copy-start | bytes 6291460
  101.9 10.2 %copy-start.4 = (bf16[32,264,132]{2,0,1:T(8,128)(2,1)}, bf16[32,264,132]{2,0,1:T(8,128)(2,1)S(1)}, u32[]{:S(2)}) copy-start(bf16[32,264,132]{2,0,1:T(8,128)(2,1)S(1)} %get-tuple-element.33) | copy-start | bytes 6690820
  101.9 10.2 %copy-start.5 = (bf16[32,264,132]{2,0,1:T(8,128)(2,1)}, bf16[32,264,132]{2,0,1:T(8,128)(2,1)S(1)}, u32[]{:S(2)}) copy-start(bf16[32,264,132]{2,0,1:T(8,128)(2,1)S(1)} %get-tuple-element.34) | copy-start | bytes 6690820
  101.9 10.2 %copy-start.13 = (bf16[32,32]{1,0:T(8,128)(2,1)S(1)}, bf16[32,32]{1,0:T(8,128)(2,1)}, u32[]{:S(2)}) copy-start(bf16[32,32]{1,0:T(8,128)(2,1)} %param.11) | copy-start | bytes 6148
  115.5 3.1 copy-start.3
  115.5 3.5 copy-start.7
  229.7 4.9 collective-permute-start.4
  232.5 7.2 %collective-permute-start.5 = (bf16[32,4,128]{2,0,1:T(8,128)(2,1)S(1)}, bf16[32,4,128]{2,0,1:T(8,128)(2,1)S(1)}, u32[]{:S(2)}, u32[]{:S(2)}) collective-permute-start(bf16[32,4,128]{2,0,1:T(8,128)(2,1)S(1)} %get-tuple-element.38), channel_id=1, source_target_pairs={{32,0},{64,32},{96,64},{128,96},{160,128},{192,160},{224,192},{256... | collective-permute-start | bytes 98312 | tf_op jit(solution)/shard_map/ppermute | solution.py:23
  251.8 10.8 %collective-permute-start.7 = (bf16[32,264,4]{1,0,2:T(8,128)(2,1)S(1)}, bf16[32,264,4]{1,0,2:T(8,128)(2,1)S(1)}, u32[]{:S(2)}, u32[]{:S(2)}) collective-permute-start(bf16[32,264,4]{1,0,2:T(8,128)(2,1)S(1)} %copy.26), channel_id=1, source_target_pairs={{0,1},{1,2},{2,3},{3,4},{4,5},{5,6},{6,7},{7,8},{8,9},{9,10},{10,1... | collective-permute-start | bytes 202760 | tf_op jit(solution)/shard_map/ppermute | solution.py:22
  253.7 5.8 collective-permute-start.6
  265.6 7.3 %copy-start.6 = (bf16[32,256,128]{2,0,1:T(8,128)(2,1)S(1)}, bf16[32,256,128]{2,0,1:T(8,128)(2,1)}, u32[]{:S(2)}) copy-start(bf16[32,256,128]{2,0,1:T(8,128)(2,1)} %get-tuple-element.50) | copy-start | bytes 6291460
  265.6 7.3 %copy-start.8 = (bf16[32,256,128]{2,0,1:T(8,128)(2,1)S(1)}, bf16[32,256,128]{2,0,1:T(8,128)(2,1)}, u32[]{:S(2)}) copy-start(bf16[32,256,128]{2,0,1:T(8,128)(2,1)} %multiply_convert_fusion.1) | copy-start | bytes 6291460
  272.9 109.6 %copy-start.9 = (bf16[256,512]{1,0:T(8,128)(2,1)S(1)}, bf16[256,512]{1,0:T(8,128)(2,1)}, u32[]{:S(2)}) copy-start(bf16[256,512]{1,0:T(8,128)(2,1)} %param.7) | copy-start | bytes 786436
  272.9 110.4 %copy-start.10 = (bf16[512,32]{0,1:T(8,128)(2,1)S(1)}, bf16[512,32]{0,1:T(8,128)(2,1)}, u32[]{:S(2)}) copy-start(bf16[512,32]{0,1:T(8,128)(2,1)} %param.8) | copy-start | bytes 98308
  272.9 227.5 %copy-start.11 = (bf16[512,32]{0,1:T(8,128)(2,1)S(1)}, bf16[512,32]{0,1:T(8,128)(2,1)}, u32[]{:S(2)}) copy-start(bf16[512,32]{0,1:T(8,128)(2,1)} %param.9) | copy-start | bytes 98308
Sparse Core Ops, SparseCore 0:
  500.5 165.3 all-reduce.3
where the time goes:
time: 675 us; the launch traced here: 674 us
  blocking collectives  365 us (54%)
  waiting for transfers between devices  176 us (26%)
  other arithmetic  39 us (6%)
  local copies, waits for them, and re-layouts  34 us (5%)
  matrix products  28.2 us (4%)
  starting transfers between devices  17 us (3%)
  between operations  14.4 us (2%)
    psum x1, waiting for transfers between devices, body(): wleft_sum, wright_sum = lax.psum((wleft_part, wright_part), 'row')  165 us
    psum x1, blocking collectives, body(): grad_left = lax.psum(left_part, 'col').astype(jnp.bfloat16)  102 us
    psum x1, blocking collectives, body(): lax.psum((kernel_part, point_part, head_part), ('row', 'col'))  96 us
    psum x1, blocking collectives, body(): column_total = lax.psum(right_part, 'row').astype(jnp.bfloat16)  80.7 us
    psum x1, blocking collectives, from_root(): return lax.psum(block, axis)  50.8 us
    all_gather x1, blocking collectives, body(): all_panels = lax.all_gather(column_total, 'col', axis=0, tiled=True)  35.4 us
    concatenate x4, other arithmetic, extended(): x = jnp.concatenate([before, x, after], axis=dim)  16.6 us
  transfers between devices with their start and end apart: 9, of which 5 were waited for; matrix products, arithmetic and copies ran while one was open for 2% of the time, Pallas kernels for 0%

commit v1 on v0

--- a/solution.py
+++ b/solution.py
@@ -135,7 +135,9 @@
     wright_part = lax.dot_general(
         bin_features, grad_right, contract, preferred_element_type=jnp.float32
     )
-    kernel_sum, point_sum, head_sum = lax.psum((kernel_part, point_part, head_part), ("row", "col"))
+    kernel_sum, point_sum, head_sum = lax.psum(
+        lax.psum((kernel_part, point_part, head_part), "col"), axis_name="row"
+    )
     wleft_sum, wright_sum = lax.psum((wleft_part, wright_part), "row")
     return (
         grad_features,

time: 675 us -> 575 us (0.85)
  blocking collectives: 365 us -> 271 us
    psum x1 -> x0, blocking collectives: 96 us -> none  [body(): lax.psum((kernel_part, point_part, head_part), ('row', 'col'))]
  transfers between devices with their start and end apart: 9 -> 9, of which waited for: 5 -> 4; matrix products, arithmetic and copies ran while one was open for 2% -> 3% of each run, Pallas kernels for 0% -> 0%
where the time goes in v1:
time: 575 us; the launch traced here: 574 us
  blocking collectives  271 us (47%)
  waiting for transfers between devices  173 us (30%)
  other arithmetic  38.8 us (7%)
  local copies, waits for them, and re-layouts  33.6 us (6%)
  matrix products  25 us (4%)
  starting transfers between devices  18.7 us (3%)
  between operations  14.4 us (3%)
    psum x1, waiting for transfers between devices, body(): wleft_sum, wright_sum = lax.psum((wleft_part, wright_part), 'row')  166 us
    psum x1, blocking collectives, body(): grad_left = lax.psum(left_part, 'col').astype(jnp.bfloat16)  105 us
    psum x1, blocking collectives, body(): column_total = lax.psum(right_part, 'row').astype(jnp.bfloat16)  79.6 us
    psum x1, blocking collectives, from_root(): return lax.psum(block, axis)  50.8 us
    all_gather x1, blocking collectives, body(): all_panels = lax.all_gather(column_total, 'col', axis=0, tiled=True)  35.4 us
    concatenate x4, other arithmetic, extended(): x = jnp.concatenate([before, x, after], axis=dim)  16.8 us
  transfers between devices with their start and end apart: 9, of which 4 were waited for; matrix products, arithmetic and copies ran while one was open for 3% of the time, Pallas kernels for 0%

profile of v1, /device:TPU:8, one launch (start us, length us, event | category | flops | bytes accessed | tf_op | source)
XLA Modules:
  0.0 573.8 jit_solution(6220135782979123154)
XLA Ops:
  8.4 50.8 %psum.77 = bf16[32,128]{1,0:T(8,128)(2,1)S(1)} all-reduce(bf16[32,128]{1,0:T(8,128)(2,1)S(1)} %fusion.34), channel_id=1, replica_groups=mesh['row'=16,'col'=32] {'row'}, use_global_device_ids=true, to_apply=%region_0.1 | all-reduce | flops 4096 | bytes 16384 | tf_op jit(solution)/shard_map/psum | solution.py:12
  64.8 3.5 multiply_convert_fusion.1
  68.3 1.9 collective-permute-done.1
  70.5 2.9 fusion.51
  73.5 3.6 copy.20
  77.1 3.6 copy.22
  80.8 1.9 collective-permute-start.3
  82.7 2.6 collective-permute-start.2
  85.3 3.3 collective-permute-done.2
  88.6 3.0 copy.21
  91.6 3.0 copy.23
  94.7 7.2 %maximum_maximum_fusion = (bf16[32,264,132]{2,0,1:T(8,128)(2,1)S(1)}, bf16[32,264,132]{2,0,1:T(8,128)(2,1)S(1)}) fusion(bf16[32,4,128]{2,0,1:T(8,128)(2,1)S(1)} %collective-permute-done.1, bf16[32,256,128]{2,0,1:T(8,128)(2,1)} %copy-done.1, bf16[32,4,128]{2,0,1:T(8,128)(2,1)S(1)} %collective-permute-done, bf16[32,264,4]{2,0,1:T(8,128)(2,1)} %copy.21, ...), kind=kLoop, calls=%fused_computation.20 | loop fusion | flops 17842176 | bytes 6758400 | tf_op jit(solution)/shard_map/concatenate | solution.py:24
  101.9 9.8 %multiply_convert_fusion = (bf16[32,256,128]{2,0,1:T(8,128)(2,1)}, f32[32,256,128]{2,0,1:T(8,128)}) fusion(bf16[32,264,132]{2,0,1:T(8,128)(2,1)S(1)} %get-tuple-element.39, f32[32]{0:T(128)S(1)} %get-tuple-element.53, bf16[32,4,128]{2,0,1:T(8,128)(2,1)S(1)} %collective-permute-done.1, bf16[32,256,128]{2,0,1:T(8,128)(2,1)S(1)} %copy-done.2, ...), kind=kLoop, calls=%fused_computation.50 | loop fusion | flops 36700160 | bytes 21087360 | tf_op jit(solution)/shard_map/convert_element_type | solution.py:82
  111.7 10.2 %fusion.23 = (f32[32]{0:T(128)S(1)}, f32[32]{0:T(128)S(1)}, f32[32]{0:T(128)S(1)}, f32[32]{0:T(128)S(1)}, f32[32]{0:T(128)S(1)}, /*index=5*/f32[32]{0:T(128)S(1)...) fusion(bf16[32,264,132]{2,0,1:T(8,128)(2,1)S(1)} %get-tuple-element.39, ...), kind=kOutput, calls=%fused_computation.47 | convolution fusion | flops 110100192 | bytes 23186560 | tf_op jit(solution)/shard_map/co,oij->cij/dot_general | solution.py:77
  122.6 4.5 collective-permute-start.4
  128.7 3.4 fusion.30
  132.2 1.7 collective-permute-done.5
  133.9 1.9 pad_maximum_fusion.3
  135.8 2.9 fusion.50
  138.7 3.6 copy.24
  142.3 3.6 copy.26
  146.0 1.9 collective-permute-start.7
  147.9 3.6 collective-permute-start.6
  151.6 2.9 convolution_bitcast_fusion.2
  154.5 3.0 copy.25
  157.6 3.0 copy.27
  160.6 7.4 %pad_maximum_fusion.1 = (bf16[32,264,132]{2,0,1:T(8,128)(2,1)S(1)}, bf16[32,264,132]{2,0,1:T(8,128)(2,1)S(1)}) fusion(bf16[32,264,4]{2,0,1:T(8,128)(2,1)} %copy.25, bf16[32,4,128]{2,0,1:T(8,128)(2,1)S(1)} %collective-permute-done.5, bf16[32,256,128]{2,0,1:T(8,128)(2,1)} %get-tuple-element.55, bf16[32,4,128]{2,0,1:T(8,128)(2,1)S(1)} %collective-permute-done.4, ...), kind=kLoop, calls=%fused_computation.22 | loop fusion | flops 17842176 | bytes 6758400 | tf_op jit(solution)/shard_map/concatenate | solution.py:24
  168.1 7.2 %fusion.48 = (f32[32,128]{1,0:T(8,128)S(1)}, f32[32,256]{0,1:T(8,128)S(1)}) fusion(bf16[32,264,132]{2,0,1:T(8,128)(2,1)S(1)} %get-tuple-element.35, f32[32]{0:T(128)S(1)} %get-tuple-element.53, bf16[32,256,128]{2,0,1:T(8,128)(2,1)S(1)} %copy-done.3, bf16[32,4,128]{2,0,1:T(8,128)(2,1)S(1)} %collective-permute-done.4, f32[32]{0:T(128)S(1)} %get-tuple-element.54, ...), kind=kLoop, calls=%fused_computation.100 | loop fusion | flops 33542144 | bytes 16893056 | tf_op jit(solution)/shard_map/reduce_sum | solution.py:116
  175.3 104.9 %all-reduce = (bf16[256,32]{1,0:T(8,128)(2,1)S(1)}, f32[9,32]{1,0:T(8,128)S(1)}, f32[32,32]{1,0:T(8,128)S(1)}, f32[32,24]{0,1:T(8,128)S(1)}) all-reduce(f32[256,32]{1,0:T(8,128)S(1)} %bitcast.73, f32[9,32]{1,0:T(8,128)S(1)} %stack.39, f32[32,32]{1,0:T(8,128)S(1)} %convolution_bitcast_fusion.2, ...), channel_id=1, replica_groups=mesh['row'=16,'col'=32] {'col'}, use_global_device_ids=true, to_apply=%region_2.3 | all-reduce | flops 10272 | bytes 65792 | tf_op jit(solution)/shard_map/psum | solution.py:123
  281.2 79.6 %all-reduce.1 = (bf16[128,32]{0,1:T(8,128)(2,1)S(1)}, f32[9,32]{1,0:T(8,128)S(1)}, f32[32,32]{1,0:T(8,128)S(1)}, f32[32,24]{0,1:T(8,128)S(1)}) all-reduce(f32[128,32]{0,1:T(8,128)S(1)} %bitcast.74, f32[9,32]{1,0:T(8,128)S(1)} %get-tuple-element.23, f32[32,32]{1,0:T(8,128)S(1)} %get-tuple-element.24, ...), channel_id=1, replica_groups=mesh['row'=16,'col'=32] {'row'}, use_global_device_ids=true, to_apply=%region_4.5 | all-reduce | flops 6176 | bytes 41216 | tf_op jit(solution)/shard_map/psum | solution.py:124
  362.0 35.4 %all_gather.3 = bf16[4096,32]{0,1:T(8,128)(2,1)S(1)} all-gather(bf16[128,32]{0,1:T(8,128)(2,1)S(1)} %get-tuple-element.26), channel_id=1, replica_groups=mesh['row'=16,'col'=32] {'col'}, dimensions={0}, use_global_device_ids=true | all-gather | bytes 270336 | tf_op jit(solution)/shard_map/all_gather | solution.py:125
  399.8 165.7 %all-reduce.5.cloned.1.call-done = (f32[512,32]{0,1:T(8,128)}, f32[512,32]{0,1:T(8,128)}) async-done(((f32[512,32]{0,1:T(8,128)}, f32[512,32]{0,1:T(8,128)}), (f32[512,32]{0,1:T(8,128)}, f32[512,32]{0,1:T(8,128)})) %all-reduce.5.cloned.1.call-update) | async-done | bytes 131088 | tf_op jit(solution)/shard_map/psum | solution.py:141
  (48 shorter events, 15.5 us)
Async XLA Ops:
  7.2 57.7 %copy-start = (bf16[24,256,128]{2,1,0:T(8,128)(2,1)S(1)}, bf16[24,256,128]{2,1,0:T(8,128)(2,1)}, u32[]{:S(2)}) copy-start(bf16[24,256,128]{2,1,0:T(8,128)(2,1)} %param.13) | copy-start | bytes 4718596
  7.2 558.3 %all-reduce.5.cloned.1.call-start = ((), (), s32[]{:S(2)}) async-start(), calls=%async_computation | async-start | bytes 262144 | tf_op jit(solution)/shard_map/psum | solution.py:141
  62.2 8.0 %copy-start.1 = (bf16[32,256,128]{2,0,1:T(8,128)(2,1)}, bf16[32,256,128]{2,0,1:T(8,128)(2,1)S(1)}, u32[]{:S(2)}) copy-start(bf16[32,256,128]{2,0,1:T(8,128)(2,1)S(1)} %add_convert_fusion) | copy-start | bytes 6291460
  62.2 6.1 %collective-permute-start = (bf16[32,4,128]{2,0,1:T(8,128)(2,1)S(1)}, bf16[32,4,128]{2,0,1:T(8,128)(2,1)S(1)}, u32[]{:S(2)}, u32[]{:S(2)}) collective-permute-start(bf16[32,4,128]{2,0,1:T(8,128)(2,1)S(1)} %get-tuple-element.44), channel_id=1, source_target_pairs={{0,32},{32,64},{64,96},{96,128},{128,160},{160,192},{192,224},{224... | collective-permute-start | bytes 98312 | tf_op jit(solution)/shard_map/ppermute | solution.py:22
  63.5 6.7 %collective-permute-start.1 = (bf16[32,4,128]{2,0,1:T(8,128)(2,1)S(1)}, bf16[32,4,128]{2,0,1:T(8,128)(2,1)S(1)}, u32[]{:S(2)}, u32[]{:S(2)}) collective-permute-start(bf16[32,4,128]{2,0,1:T(8,128)(2,1)S(1)} %get-tuple-element.45), channel_id=1, source_target_pairs={{32,0},{64,32},{96,64},{128,96},{160,128},{192,160},{224,192},{256... | collective-permute-start | bytes 98312 | tf_op jit(solution)/shard_map/ppermute | solution.py:23
  73.5 11.8 %copy-start.8 = (f32[9,32]{1,0:T(8,128)S(1)}, f32[9,32]{1,0:T(8,128)}, u32[]{:S(2)}) copy-start(f32[9,32]{1,0:T(8,128)} %param.10) | copy-start | bytes 3460
  80.8 10.9 %collective-permute-start.3 = (bf16[32,264,4]{1,0,2:T(8,128)(2,1)S(1)}, bf16[32,264,4]{1,0,2:T(8,128)(2,1)S(1)}, u32[]{:S(2)}, u32[]{:S(2)}) collective-permute-start(bf16[32,264,4]{1,0,2:T(8,128)(2,1)S(1)} %copy.22), channel_id=1, source_target_pairs={{1,0},{2,1},{3,2},{4,3},{5,4},{6,5},{7,6},{8,7},{9,8},{10,9},{11,1... | collective-permute-start | bytes 202760 | tf_op jit(solution)/shard_map/ppermute | solution.py:23
  82.7 5.9 %collective-permute-start.2 = (bf16[32,264,4]{1,0,2:T(8,128)(2,1)S(1)}, bf16[32,264,4]{1,0,2:T(8,128)(2,1)S(1)}, u32[]{:S(2)}, u32[]{:S(2)}) collective-permute-start(bf16[32,264,4]{1,0,2:T(8,128)(2,1)S(1)} %copy.20), channel_id=1, source_target_pairs={{0,1},{1,2},{2,3},{3,4},{4,5},{5,6},{6,7},{7,8},{8,9},{9,10},{10,1... | collective-permute-start | bytes 202760 | tf_op jit(solution)/shard_map/ppermute | solution.py:22
  94.7 7.2 %copy-start.2 = (bf16[32,256,128]{2,0,1:T(8,128)(2,1)S(1)}, bf16[32,256,128]{2,0,1:T(8,128)(2,1)}, u32[]{:S(2)}) copy-start(bf16[32,256,128]{2,0,1:T(8,128)(2,1)} %copy-done.1) | copy-start | bytes 6291460
  101.9 9.8 %copy-start.9 = (bf16[32,32]{1,0:T(8,128)(2,1)S(1)}, bf16[32,32]{1,0:T(8,128)(2,1)}, u32[]{:S(2)}) copy-start(bf16[32,32]{1,0:T(8,128)(2,1)} %param.11) | copy-start | bytes 6148
  122.6 9.5 %collective-permute-start.4 = (bf16[32,4,128]{2,0,1:T(8,128)(2,1)S(1)}, bf16[32,4,128]{2,0,1:T(8,128)(2,1)S(1)}, u32[]{:S(2)}, u32[]{:S(2)}) collective-permute-start(bf16[32,4,128]{2,0,1:T(8,128)(2,1)S(1)} %get-tuple-element.42), channel_id=1, source_target_pairs={{0,32},{32,64},{64,96},{96,128},{128,160},{160,192},{192,224},{224... | collective-permute-start | bytes 98312 | tf_op jit(solution)/shard_map/ppermute | solution.py:22
  127.2 6.7 %collective-permute-start.5 = (bf16[32,4,128]{2,0,1:T(8,128)(2,1)S(1)}, bf16[32,4,128]{2,0,1:T(8,128)(2,1)S(1)}, u32[]{:S(2)}, u32[]{:S(2)}) collective-permute-start(bf16[32,4,128]{2,0,1:T(8,128)(2,1)S(1)} %get-tuple-element.43), channel_id=1, source_target_pairs={{32,0},{64,32},{96,64},{128,96},{160,128},{192,160},{224,192},{256... | collective-permute-start | bytes 98312 | tf_op jit(solution)/shard_map/ppermute | solution.py:23
  146.0 11.6 %collective-permute-start.7 = (bf16[32,264,4]{1,0,2:T(8,128)(2,1)S(1)}, bf16[32,264,4]{1,0,2:T(8,128)(2,1)S(1)}, u32[]{:S(2)}, u32[]{:S(2)}) collective-permute-start(bf16[32,264,4]{1,0,2:T(8,128)(2,1)S(1)} %copy.26), channel_id=1, source_target_pairs={{0,1},{1,2},{2,3},{3,4},{4,5},{5,6},{6,7},{7,8},{8,9},{9,10},{10,1... | collective-permute-start | bytes 202760 | tf_op jit(solution)/shard_map/ppermute | solution.py:22
  147.9 6.6 %collective-permute-start.6 = (bf16[32,264,4]{1,0,2:T(8,128)(2,1)S(1)}, bf16[32,264,4]{1,0,2:T(8,128)(2,1)S(1)}, u32[]{:S(2)}, u32[]{:S(2)}) collective-permute-start(bf16[32,264,4]{1,0,2:T(8,128)(2,1)S(1)} %copy.24), channel_id=1, source_target_pairs={{1,0},{2,1},{3,2},{4,3},{5,4},{6,5},{7,6},{8,7},{9,8},{10,9},{11,1... | collective-permute-start | bytes 202760 | tf_op jit(solution)/shard_map/ppermute | solution.py:23
  160.6 7.4 %copy-start.3 = (bf16[32,256,128]{2,0,1:T(8,128)(2,1)S(1)}, bf16[32,256,128]{2,0,1:T(8,128)(2,1)}, u32[]{:S(2)}) copy-start(bf16[32,256,128]{2,0,1:T(8,128)(2,1)} %get-tuple-element.55) | copy-start | bytes 6291460
  160.6 7.4 %copy-start.4 = (bf16[32,256,128]{2,0,1:T(8,128)(2,1)S(1)}, bf16[32,256,128]{2,0,1:T(8,128)(2,1)}, u32[]{:S(2)}) copy-start(bf16[32,256,128]{2,0,1:T(8,128)(2,1)} %multiply_convert_fusion.1) | copy-start | bytes 6291460
  168.0 112.1 %copy-start.5 = (bf16[256,512]{1,0:T(8,128)(2,1)S(1)}, bf16[256,512]{1,0:T(8,128)(2,1)}, u32[]{:S(2)}) copy-start(bf16[256,512]{1,0:T(8,128)(2,1)} %param.7) | copy-start | bytes 786436
  168.1 112.9 %copy-start.6 = (bf16[512,32]{0,1:T(8,128)(2,1)S(1)}, bf16[512,32]{0,1:T(8,128)(2,1)}, u32[]{:S(2)}) copy-start(bf16[512,32]{0,1:T(8,128)(2,1)} %param.8) | copy-start | bytes 98308
  168.1 230.1 %copy-start.7 = (bf16[512,32]{0,1:T(8,128)(2,1)S(1)}, bf16[512,32]{0,1:T(8,128)(2,1)}, u32[]{:S(2)}) copy-start(bf16[512,32]{0,1:T(8,128)(2,1)} %param.9) | copy-start | bytes 98308
Sparse Core Ops, SparseCore 0:
  399.3 166.0 all-reduce.4
